TPU v7x, 32 devices: a whole 2x2x4 slice. The times are simulated.
32 devices in a mesh: leaf: 8 (over y, x, core), front: 4 (over z).
Axes of the slice: x: 2, y: 2, z: 4, core: 2. Of those that a mesh axis runs over, the one named last changes fastest.
Arguments:
- leaf_rhs: float32 [8, 64, 256], P('leaf', None, 'front'), may hold values from -6 to 6
- sep_rhs: float32 [8, 64, 256], P('leaf', None, 'front'), may hold values from -6 to 6
- leaf_inverse: float32 [8, 256, 256], P('leaf', 'front'), as said below
- sep_inverse: float32 [8, 256, 256], P('leaf', 'front')
- leaf_block: float32 [8, 32, 256], P('leaf', None, 'front'), may hold values from -0.375 to 0.375
- sep_block: float32 [8, 32, 256], P('leaf', None, 'front'), may hold values from -0.375 to 0.375
- pattern: int32 [2, 8, 32], replicated, may hold values from 0 to 255, as said below
- outer_solution: float32 [64, 256], P(None, 'front'), may hold values from -6 to 6
Outputs:
- solution: float32 [2, 8, 64, 256], P(None, 'leaf', None, 'front')
Inputs may be any that keep to these rules, and one draw needn't show every extreme that they name: `pattern`: within one supernode the 32 entries are distinct and rising, the first is 0 and the last is 255. `leaf_inverse`: each leaf block is lower triangular with its diagonal bounded away from zero.
All inputs are finite; a program needn't handle non-finite values.
Results may differ from a plain program's by a relative error of at most 0.0003.
Values sent between devices are 32-bit elements; how exact they have to be, the bound alone decides.
No kernel may reach another device: no remote copies, remote signals or barrier semaphores. Data moves between devices by JAX's collectives and lax.ppermute only.
A program may use at most 64 MiB of HBM per device.

v0:
```python
import jax
import jax.numpy as jnp
from jax import lax
from jax.sharding import PartitionSpec as P


def partner(block, axis, distance):
    count = lax.axis_size(axis)
    route = []
    for low in range(count):
        high = low | 1 << distance
        if high != low and high < count:
            route += [(low, high), (high, low)]
    return lax.ppermute(block, axis, route)


def times_rows(vectors, matrix):
    return jnp.dot(
        vectors, matrix, precision=lax.Precision.HIGHEST, preferred_element_type=jnp.float32
    )


def against_rows(vectors, matrix):
    return lax.dot_general(
        vectors,
        matrix,
        (((1,), (1,)), ((), ())),
        precision=lax.Precision.HIGHEST,
        preferred_element_type=jnp.float32,
    )


def body(
    leaf_rhs, sep_rhs, leaf_inverse, sep_inverse, leaf_block, sep_block, pattern, outer_solution
):
    group_count = lax.axis_size("leaf")
    depth = group_count.bit_length() - 1
    group_pos = lax.axis_index("leaf")
    front_pos = lax.axis_index("front")
    local_rows = leaf_rhs.shape[-1]
    full_rows = leaf_inverse.shape[-1]
    vector_count = leaf_rhs.shape[1]
    leaf_r = leaf_rhs[0]
    leaf_inv = leaf_inverse[0]
    leaf_u = leaf_block[0]
    sep_r = sep_rhs[0]
    sep_inv = sep_inverse[0]
    sep_u = sep_block[0]
    all_rows = jnp.arange(full_rows, dtype=jnp.int32)

    def geometry(level):
        blocks = 2 ** min(level, depth)
        share = local_rows // blocks
        offset = local_rows - (local_rows >> level - 1)
        return (share, offset, group_pos % blocks)

    def label_of(level):
        if level > depth:
            return jnp.int32(0)
        return group_pos // 2**level * 2**level + 2 ** (level - 1)

    def ids_of(level):
        return lax.dynamic_index_in_dim(pattern[1], label_of(level), 0, keepdims=False)

    def block_sum(term, level):
        nbits = min(level, depth)
        if nbits == depth:
            return lax.psum(term, ("leaf", "front"))
        piece = lax.psum_scatter(term, "front", scatter_dimension=1, tiled=True)
        for bit in range(nbits):
            piece = piece + partner(piece, "leaf", bit)
        return lax.all_gather(piece, "front", axis=1, tiled=True)

    leaf_y = against_rows(lax.all_gather(leaf_r, "front", axis=1, tiled=True), leaf_inv)
    leaf_ids = lax.dynamic_index_in_dim(pattern[0], group_pos, 0, keepdims=False)
    child_part = against_rows(leaf_y, leaf_u)
    child_ids = leaf_ids
    solved = {}
    for level in range(1, depth + 2):
        share, offset, inner_pos = geometry(level)
        own_r = sep_r[:, offset : offset + share]
        start_col = front_pos * local_rows + inner_pos * share
        contribution = jnp.zeros((vector_count, full_rows), jnp.float32)
        contribution = lax.dynamic_update_slice(contribution, own_r, (jnp.int32(0), start_col))
        selector = (child_ids[:, None] == all_rows[None, :]).astype(jnp.float32)
        contribution = contribution - times_rows(child_part, selector)
        whole_v = block_sum(contribution, level)
        y_level = against_rows(whole_v, sep_inv[offset : offset + share, :])
        solved[level] = y_level
        if level <= depth:
            child_part = against_rows(y_level, sep_u[:, offset : offset + share])
            child_ids = ids_of(level)
    parent_x = lax.all_gather(outer_solution, "front", axis=1, tiled=True)
    sep_full = jnp.zeros((vector_count, full_rows), jnp.float32)
    for level in range(depth + 1, 0, -1):
        share, offset, inner_pos = geometry(level)
        picked = jnp.take(parent_x, ids_of(level), axis=1)
        rest = solved[level] - times_rows(picked, sep_u[:, offset : offset + share])
        term = times_rows(rest, sep_inv[offset : offset + share, :])
        parent_x = block_sum(term, level)
        sep_full = jnp.where(label_of(level) == group_pos, parent_x, sep_full)
    picked = jnp.take(parent_x, leaf_ids, axis=1)
    rest = leaf_y - times_rows(picked, leaf_u)
    leaf_x = lax.psum_scatter(times_rows(rest, leaf_inv), "front", scatter_dimension=1, tiled=True)
    sep_x = lax.dynamic_slice_in_dim(sep_full, front_pos * local_rows, local_rows, 1)
    return jnp.stack([leaf_x, sep_x])[:, None]


def solution(mesh):
    placed = (
        P("leaf", None, "front"),
        P("leaf", None, "front"),
        P("leaf", "front", None),
        P("leaf", "front", None),
        P("leaf", None, "front"),
        P("leaf", None, "front"),
        P(),
        P(None, "front"),
    )
    return jax.shard_map(
        body, mesh=mesh, in_specs=placed, out_specs=P(None, "leaf", None, "front"), check_vma=False
    )
```

profile of v0, /device:TPU:0, one launch (start us, length us, event | category | flops | bytes accessed | tf_op | source)
XLA Modules:
  0.0 694.5 jit_solution(14276887811836147891)
XLA Ops:
  7.4 15.1 %all-gather = f32[1,64,256]{1,0,2:T(1,128)S(1)} all-gather(f32[1,64,64]{1,0,2:T(1,128)S(1)} %copy.15), channel_id=2, replica_groups=mesh['leaf'=8,'front'=4] {'front'}, dimensions={2}, use_global_device_ids=true | all-gather | bytes 81920 | tf_op jit(solution)/shard_map/all_gather | solution.py:74
  25.6 20.6 %reduce-scatter.16.cloned.1.call-done = f32[64,64]{1,0:T(8,128)} async-done(((f32[256,64]{1,0:T(8,128)}), f32[64,64]{1,0:T(8,128)}) %reduce-scatter.16.cloned.1.call-update) | async-done | bytes 16400
  48.4 13.5 %all_gather.19 = f32[64,256]{0,1:T(8,128)S(1)} all-gather(f32[64,64]{0,1:T(8,128)S(1)} %copy.16), channel_id=1, replica_groups=mesh['leaf'=8,'front'=4] {'front'}, dimensions={1}, use_global_device_ids=true | all-gather | bytes 81920 | tf_op jit(solution)/shard_map/all_gather | solution.py:72
  64.0 17.4 %reduce-scatter.18.cloned.1.call-done = f32[64,64]{1,0:T(8,128)} async-done(((f32[256,64]{1,0:T(8,128)}), f32[64,64]{1,0:T(8,128)}) %reduce-scatter.18.cloned.1.call-update) | async-done | bytes 16400
  82.3 1.2 collective-permute-done.1
  83.5 1.5 collective-permute-start.2
  85.5 2.0 collective-permute-done.2
  87.5 13.4 %all_gather.20 = f32[64,256]{0,1:T(8,128)S(1)} all-gather(f32[64,64]{0,1:T(8,128)S(1)} %copy.17), channel_id=1, replica_groups=mesh['leaf'=8,'front'=4] {'front'}, dimensions={1}, use_global_device_ids=true | all-gather | bytes 81920 | tf_op jit(solution)/shard_map/all_gather | solution.py:72
  102.8 115.3 %all-reduce.5.cloned.1.call-done = f32[64,256]{1,0:T(8,128)} async-done(((f32[64,256]{1,0:T(8,128)}), f32[64,256]{1,0:T(8,128)}) %all-reduce.5.cloned.1.call-update) | async-done | bytes 65552 | tf_op jit(solution)/shard_map/psum | solution.py:68
  221.0 14.3 %all_gather.21 = f32[64,256]{0,1:T(8,128)S(1)} all-gather(f32[64,64]{0,1:T(8,128)S(1)} %copy.18), channel_id=1, replica_groups=mesh['leaf'=8,'front'=4] {'front'}, dimensions={1}, use_global_device_ids=true | all-gather | bytes 81920 | tf_op jit(solution)/shard_map/all_gather | solution.py:93
  235.9 105.9 %all-reduce.7.cloned.1.call-done = f32[64,256]{1,0:T(8,128)} async-done(((f32[64,256]{1,0:T(8,128)}), f32[64,256]{1,0:T(8,128)}) %all-reduce.7.cloned.1.call-update) | async-done | bytes 65552 | tf_op jit(solution)/shard_map/psum | solution.py:68
  344.1 121.5 %all-reduce.9.cloned.1.call-done = f32[64,256]{1,0:T(8,128)} async-done(((f32[64,256]{1,0:T(8,128)}), f32[64,256]{1,0:T(8,128)}) %all-reduce.9.cloned.1.call-update) | async-done | bytes 65552 | tf_op jit(solution)/shard_map/psum | solution.py:68
  468.4 121.0 %all-reduce.11.cloned.1.call-done = f32[64,256]{1,0:T(8,128)} async-done(((f32[64,256]{1,0:T(8,128)}), f32[64,256]{1,0:T(8,128)}) %all-reduce.11.cloned.1.call-update) | async-done | bytes 65552 | tf_op jit(solution)/shard_map/psum | solution.py:68
  591.2 1.1 convolution_bitcast_fusion.2
  592.4 20.0 %reduce-scatter.20.cloned.1.call-done = f32[64,64]{1,0:T(8,128)} async-done(((f32[256,64]{1,0:T(8,128)}), f32[64,64]{1,0:T(8,128)}) %reduce-scatter.20.cloned.1.call-update) | async-done | bytes 16400
  613.3 1.2 collective-permute-done.3
  614.5 1.6 collective-permute-start.4
  616.0 2.3 collective-permute-done.4
  618.5 13.3 %all_gather.22 = f32[64,256]{0,1:T(8,128)S(1)} all-gather(f32[64,64]{0,1:T(8,128)S(1)} %copy.21), channel_id=1, replica_groups=mesh['leaf'=8,'front'=4] {'front'}, dimensions={1}, use_global_device_ids=true | all-gather | bytes 81920 | tf_op jit(solution)/shard_map/all_gather | solution.py:72
  632.6 1.0 convolution_bitcast_fusion.1
  633.8 17.6 %reduce-scatter.22.cloned.1.call-done = f32[64,64]{1,0:T(8,128)} async-done(((f32[256,64]{1,0:T(8,128)}), f32[64,64]{1,0:T(8,128)}) %reduce-scatter.22.cloned.1.call-update) | async-done | bytes 16400
  652.3 1.1 collective-permute-done.5
  653.5 13.4 %all_gather.23 = f32[64,256]{0,1:T(8,128)S(1)} all-gather(f32[64,64]{0,1:T(8,128)S(1)} %copy.22), channel_id=1, replica_groups=mesh['leaf'=8,'front'=4] {'front'}, dimensions={1}, use_global_device_ids=true | all-gather | bytes 81920 | tf_op jit(solution)/shard_map/all_gather | solution.py:72
  669.9 16.6 %reduce-scatter.24.cloned.1.call-done = f32[64,64]{1,0:T(8,128)} async-done(((f32[256,64]{1,0:T(8,128)}), f32[64,64]{1,0:T(8,128)}) %reduce-scatter.24.cloned.1.call-update) | async-done | bytes 16400
  (119 shorter events, 28.9 us)
Async XLA Ops:
  6.5 15.9 %copy-start = (f32[1,64,256]{2,1,0:T(8,128)S(1)}, f32[1,64,256]{2,1,0:T(8,128)}, u32[]{:S(2)}) copy-start(f32[1,64,256]{2,1,0:T(8,128)} %param.12) | copy-start | bytes 196612
  6.5 0.8 copy-start.7
  6.5 39.7 %reduce-scatter.16.cloned.1.call-start = ((), (), s32[]{:S(2)}) async-start(), calls=%async_computation.9 | async-start | bytes 163840
  6.5 0.7 copy-start.9
  22.5 0.7 copy-start.6
  23.4 0.8 copy-start.1
  25.5 55.9 %reduce-scatter.18.cloned.1.call-start = ((), (), s32[]{:S(2)}) async-start(), calls=%async_computation.10 | async-start | bytes 163840
  47.0 1.3 collective-permute-start
  48.4 13.5 %copy-start.3 = (f32[1,64,256]{2,1,0:T(8,128)S(1)}, f32[1,64,256]{2,1,0:T(8,128)}, u32[]{:S(2)}) copy-start(f32[1,64,256]{2,1,0:T(8,128)} %param.13) | copy-start | bytes 196612
  63.9 154.2 %all-reduce.5.cloned.1.call-start = ((), (), s32[]{:S(2)}) async-start(), calls=%async_computation.5 | async-start | bytes 131072 | tf_op jit(solution)/shard_map/psum | solution.py:68
  82.2 1.3 collective-permute-start.1
  83.5 3.9 collective-permute-start.2
  102.3 239.6 %all-reduce.7.cloned.1.call-start = ((), (), s32[]{:S(2)}) async-start(), calls=%async_computation.6 | async-start | bytes 131072 | tf_op jit(solution)/shard_map/psum | solution.py:68
  220.2 0.8 copy-start.8
  220.2 245.4 %all-reduce.9.cloned.1.call-start = ((), (), s32[]{:S(2)}) async-start(), calls=%async_computation.7 | async-start | bytes 131072 | tf_op jit(solution)/shard_map/psum | solution.py:68
  344.0 245.4 %all-reduce.11.cloned.1.call-start = ((), (), s32[]{:S(2)}) async-start(), calls=%async_computation.8 | async-start | bytes 131072 | tf_op jit(solution)/shard_map/psum | solution.py:68
  468.4 144.0 %reduce-scatter.20.cloned.1.call-start = ((), (), s32[]{:S(2)}) async-start(), calls=%async_computation.11 | async-start | bytes 163840
  592.3 59.0 %reduce-scatter.22.cloned.1.call-start = ((), (), s32[]{:S(2)}) async-start(), calls=%async_computation.12 | async-start | bytes 163840
  613.2 1.3 collective-permute-start.3
  614.5 3.9 collective-permute-start.4
  633.7 52.8 %reduce-scatter.24.cloned.1.call-start = ((), (), s32[]{:S(2)}) async-start(), calls=%async_computation.13 | async-start | bytes 163840
  652.2 1.3 collective-permute-start.5
  668.9 0.8 copy-start.4
  668.9 0.9 copy-start.5
  (1 other events, 0.7 us)
Sparse Core Ops, SparseCore 0:
  25.6 20.5 reduce-scatter.15
  64.0 17.3 reduce-scatter.17
  102.4 115.6 all-reduce.4
  223.5 118.3 all-reduce.6
  347.3 118.3 all-reduce.8
  471.1 118.3 all-reduce.10
  592.4 19.9 reduce-scatter.19
  633.8 17.4 reduce-scatter.21
  669.1 17.4 reduce-scatter.23
where the time goes:
time: 696 us; the launch traced here: 695 us
  waiting for transfers between devices  565 us (81%)
  blocking collectives  83.1 us (12%)
  local copies, waits for them, and re-layouts  16.8 us (2%)
  between operations  13.6 us (2%)
  matrix products  12.1 us (2%)
    psum x4, waiting for transfers between devices, block_sum(): return lax.psum(term, ('leaf', 'front'))  464 us
    unnamed x14, waiting for transfers between devices  92.4 us
    all_gather x4, blocking collectives, block_sum(): return lax.all_gather(piece, 'front', axis=1, tiled=True)  53.7 us
    all_gather x1, blocking collectives, body(): lax.all_gather(leaf_r, 'front', axis=1, tiled=True)  15.1 us
    all_gather x1, blocking collectives, body(): parent_x = lax.all_gather(outer_solution, 'front', axis=1, tiled=True)  14.3 us
  transfers between devices with their start and end apart: 15, of which 15 were waited for; matrix products, arithmetic and copies ran while one was open for 0% of the time, Pallas kernels for 0%

commit v1 on v0

--- a/solution.py
+++ b/solution.py
@@ -65,7 +65,10 @@
     def block_sum(term, level):
         nbits = min(level, depth)
         if nbits == depth:
-            return lax.psum(term, ("leaf", "front"))
+            levels_all_carry = lambda own_rows: lax.all_gather(own_rows, ("leaf", "front")).sum(
+                axis=0
+            )
+            return levels_all_carry(term)
         piece = lax.psum_scatter(term, "front", scatter_dimension=1, tiled=True)
         for bit in range(nbits):
             piece = piece + partner(piece, "leaf", bit)

time: 696 us -> 440 us (0.63)
  waiting for transfers between devices: 565 us -> 305 us
  other arithmetic: 0.85 us -> 8.43 us
    psum x4 -> x0, waiting for transfers between devices: 464 us -> none  [block_sum(): return lax.psum(term, ('leaf', 'front'))]
    all_gather x0 -> x4, waiting for transfers between devices: none -> 206 us  [block_sum(): lax.all_gather(own_rows, ('leaf', 'front')).sum(axis=0)]
  transfers between devices with their start and end apart: 15 -> 15, of which waited for: 15 -> 14; matrix products, arithmetic and copies ran while one was open for 0% -> 1% of each run, Pallas kernels for 0% -> 0%
where the time goes in v1:
time: 440 us; the launch traced here: 439 us
  waiting for transfers between devices  305 us (69%)
  blocking collectives  82.1 us (19%)
  local copies, waits for them, and re-layouts  14.1 us (3%)
  between operations  13.7 us (3%)
  matrix products  11.9 us (3%)
  other arithmetic  8.43 us (2%)
    all_gather x4, waiting for transfers between devices, block_sum(): lax.all_gather(own_rows, ('leaf', 'front')).sum(axis=0)  206 us
    unnamed x14, waiting for transfers between devices  91.4 us
    all_gather x4, blocking collectives, block_sum(): return lax.all_gather(piece, 'front', axis=1, tiled=True)  53.7 us
    all_gather x1, blocking collectives, body(): lax.all_gather(leaf_r, 'front', axis=1, tiled=True)  15.1 us
    all_gather x1, blocking collectives, body(): parent_x = lax.all_gather(outer_solution, 'front', axis=1, tiled=True)  13.4 us
  transfers between devices with their start and end apart: 15, of which 14 were waited for; matrix products, arithmetic and copies ran while one was open for 1% of the time, Pallas kernels for 0%

profile of v1, /device:TPU:0, one launch (start us, length us, event | category | flops | bytes accessed | tf_op | source)
XLA Modules:
  0.0 438.9 jit_solution(15576504019177610010)
XLA Ops:
  8.2 15.1 %all-gather = f32[1,64,256]{1,0,2:T(1,128)S(1)} all-gather(f32[1,64,64]{1,0,2:T(1,128)S(1)} %copy.15), channel_id=2, replica_groups=mesh['leaf'=8,'front'=4] {'front'}, dimensions={2}, use_global_device_ids=true | all-gather | bytes 81920 | tf_op jit(solution)/shard_map/all_gather | solution.py:77
  26.7 20.7 %reduce-scatter.16.cloned.1.call-done = f32[64,64]{1,0:T(8,128)} async-done(((f32[256,64]{1,0:T(8,128)}), f32[64,64]{1,0:T(8,128)}) %reduce-scatter.16.cloned.1.call-update) | async-done | bytes 16400
  49.7 13.5 %all_gather.43 = f32[64,256]{0,1:T(8,128)S(1)} all-gather(f32[64,64]{0,1:T(8,128)S(1)} %copy.16), channel_id=1, replica_groups=mesh['leaf'=8,'front'=4] {'front'}, dimensions={1}, use_global_device_ids=true | all-gather | bytes 81920 | tf_op jit(solution)/shard_map/all_gather | solution.py:75
  65.6 17.6 %reduce-scatter.18.cloned.1.call-done = f32[64,64]{1,0:T(8,128)} async-done(((f32[256,64]{1,0:T(8,128)}), f32[64,64]{1,0:T(8,128)}) %reduce-scatter.18.cloned.1.call-update) | async-done | bytes 16400
  84.0 1.2 collective-permute-done.1
  85.2 1.5 collective-permute-start.2
  87.2 1.9 collective-permute-done.2
  89.2 13.3 %all_gather.44 = f32[64,256]{0,1:T(8,128)S(1)} all-gather(f32[64,64]{0,1:T(8,128)S(1)} %copy.17), channel_id=1, replica_groups=mesh['leaf'=8,'front'=4] {'front'}, dimensions={1}, use_global_device_ids=true | all-gather | bytes 81920 | tf_op jit(solution)/shard_map/all_gather | solution.py:75
  104.4 54.4 %all-gather.10.cloned.1.call-done = f32[2048,256]{1,0:T(8,128)} async-done(((f32[64,256]{1,0:T(8,128)}), f32[2048,256]{1,0:T(8,128)}) %all-gather.10.cloned.1.call-update) | async-done | bytes 2097168 | tf_op jit(solution)/shard_map/all_gather | solution.py:68
  158.8 1.7 reduce_sum.36
  162.0 13.4 %all_gather.49 = f32[64,256]{0,1:T(8,128)S(1)} all-gather(f32[64,64]{0,1:T(8,128)S(1)} %copy.18), channel_id=1, replica_groups=mesh['leaf'=8,'front'=4] {'front'}, dimensions={1}, use_global_device_ids=true | all-gather | bytes 81920 | tf_op jit(solution)/shard_map/all_gather | solution.py:96
  176.6 40.7 %all-gather.12.cloned.1.call-done = f32[2048,256]{1,0:T(8,128)} async-done(((f32[64,256]{1,0:T(8,128)}), f32[2048,256]{1,0:T(8,128)}) %all-gather.12.cloned.1.call-update) | async-done | bytes 2097168 | tf_op jit(solution)/shard_map/all_gather | solution.py:68
  217.3 1.7 reduce_sum.37
  220.5 55.4 %all-gather.14.cloned.1.call-done = f32[2048,256]{1,0:T(8,128)} async-done(((f32[64,256]{1,0:T(8,128)}), f32[2048,256]{1,0:T(8,128)}) %all-gather.14.cloned.1.call-update) | async-done | bytes 2097168 | tf_op jit(solution)/shard_map/all_gather | solution.py:68
  275.9 1.7 reduce_sum.38
  279.5 55.4 %all-gather.16.cloned.1.call-done = f32[2048,256]{1,0:T(8,128)} async-done(((f32[64,256]{1,0:T(8,128)}), f32[2048,256]{1,0:T(8,128)}) %all-gather.16.cloned.1.call-update) | async-done | bytes 2097168 | tf_op jit(solution)/shard_map/all_gather | solution.py:68
  335.0 1.7 reduce_sum.39
  338.8 18.1 %reduce-scatter.20.cloned.1.call-done = f32[64,64]{1,0:T(8,128)} async-done(((f32[256,64]{1,0:T(8,128)}), f32[64,64]{1,0:T(8,128)}) %reduce-scatter.20.cloned.1.call-update) | async-done | bytes 16400
  359.0 1.5 collective-permute-start.4
  360.5 2.4 collective-permute-done.4
  363.0 13.3 %all_gather.54 = f32[64,256]{0,1:T(8,128)S(1)} all-gather(f32[64,64]{0,1:T(8,128)S(1)} %copy.21), channel_id=1, replica_groups=mesh['leaf'=8,'front'=4] {'front'}, dimensions={1}, use_global_device_ids=true | all-gather | bytes 81920 | tf_op jit(solution)/shard_map/all_gather | solution.py:75
  378.3 17.5 %reduce-scatter.22.cloned.1.call-done = f32[64,64]{1,0:T(8,128)} async-done(((f32[256,64]{1,0:T(8,128)}), f32[64,64]{1,0:T(8,128)}) %reduce-scatter.22.cloned.1.call-update) | async-done | bytes 16400
  398.0 13.4 %all_gather.55 = f32[64,256]{0,1:T(8,128)S(1)} all-gather(f32[64,64]{0,1:T(8,128)S(1)} %copy.22), channel_id=1, replica_groups=mesh['leaf'=8,'front'=4] {'front'}, dimensions={1}, use_global_device_ids=true | all-gather | bytes 81920 | tf_op jit(solution)/shard_map/all_gather | solution.py:75
  413.5 17.4 %reduce-scatter.24.cloned.1.call-done = f32[64,64]{1,0:T(8,128)} async-done(((f32[256,64]{1,0:T(8,128)}), f32[64,64]{1,0:T(8,128)}) %reduce-scatter.24.cloned.1.call-update) | async-done | bytes 16400
  (115 shorter events, 30.6 us)
Async XLA Ops:
  6.5 16.7 %copy-start = (f32[1,64,256]{2,1,0:T(8,128)S(1)}, f32[1,64,256]{2,1,0:T(8,128)}, u32[]{:S(2)}) copy-start(f32[1,64,256]{2,1,0:T(8,128)} %param.12) | copy-start | bytes 196612
  6.5 80.2 %copy-start.1 = (f32[1,64,64]{2,1,0:T(8,128)S(1)}, f32[1,64,64]{2,1,0:T(8,128)}, u32[]{:S(2)}) copy-start(f32[1,64,64]{2,1,0:T(8,128)} %param.11) | copy-start | bytes 49156
  6.5 96.0 %copy-start.3 = (f32[1,64,256]{2,1,0:T(8,128)S(1)}, f32[1,64,256]{2,1,0:T(8,128)}, u32[]{:S(2)}) copy-start(f32[1,64,256]{2,1,0:T(8,128)} %param.13) | copy-start | bytes 196612
  6.5 57.7 %copy-start.2 = (f32[1,32,64]{2,1,0:T(8,128)S(1)}, f32[1,32,64]{2,1,0:T(8,128)}, u32[]{:S(2)}) copy-start(f32[1,32,64]{2,1,0:T(8,128)} %param.15) | copy-start | bytes 24580
  6.5 40.8 %reduce-scatter.16.cloned.1.call-start = ((), (), s32[]{:S(2)}) async-start(), calls=%async_computation.9 | async-start | bytes 163840
  26.6 56.5 %reduce-scatter.18.cloned.1.call-start = ((), (), s32[]{:S(2)}) async-start(), calls=%async_computation.10 | async-start | bytes 163840
  48.2 1.4 collective-permute-start
  64.7 97.2 %copy-start.5 = (f32[64,64]{1,0:T(8,128)S(1)}, f32[64,64]{1,0:T(8,128)}, u32[]{:S(2)}) copy-start(f32[64,64]{1,0:T(8,128)} %param.17) | copy-start | bytes 49156
  65.5 93.3 %all-gather.10.cloned.1.call-start = ((), (), s32[]{:S(2)}) async-start(), calls=%async_computation.5 | async-start | bytes 2162688 | tf_op jit(solution)/shard_map/all_gather | solution.py:68
  84.0 1.3 collective-permute-start.1
  85.2 3.9 collective-permute-start.2
  103.9 113.4 %all-gather.12.cloned.1.call-start = ((), (), s32[]{:S(2)}) async-start(), calls=%async_computation.6 | async-start | bytes 2162688 | tf_op jit(solution)/shard_map/all_gather | solution.py:68
  161.8 114.1 %all-gather.14.cloned.1.call-start = ((), (), s32[]{:S(2)}) async-start(), calls=%async_computation.7 | async-start | bytes 2162688 | tf_op jit(solution)/shard_map/all_gather | solution.py:68
  220.4 114.6 %all-gather.16.cloned.1.call-start = ((), (), s32[]{:S(2)}) async-start(), calls=%async_computation.8 | async-start | bytes 2162688 | tf_op jit(solution)/shard_map/all_gather | solution.py:68
  279.5 77.4 %reduce-scatter.20.cloned.1.call-start = ((), (), s32[]{:S(2)}) async-start(), calls=%async_computation.11 | async-start | bytes 163840
  335.0 77.0 %copy-start.4 = (f32[1,32,64]{2,1,0:T(8,128)S(1)}, f32[1,32,64]{2,1,0:T(8,128)}, u32[]{:S(2)}) copy-start(f32[1,32,64]{2,1,0:T(8,128)} %param.14) | copy-start | bytes 24580
  338.7 57.1 %reduce-scatter.22.cloned.1.call-start = ((), (), s32[]{:S(2)}) async-start(), calls=%async_computation.12 | async-start | bytes 163840
  357.7 1.3 collective-permute-start.3
  359.0 3.9 collective-permute-start.4
  378.2 52.7 %reduce-scatter.24.cloned.1.call-start = ((), (), s32[]{:S(2)}) async-start(), calls=%async_computation.13 | async-start | bytes 163840
  396.6 1.3 collective-permute-start.5
Sparse Core Ops, SparseCore 0:
  26.7 20.6 reduce-scatter.15
  65.6 17.4 reduce-scatter.17
  104.0 54.7 all-gather.9
  161.9 55.3 all-gather.11
  220.5 55.3 all-gather.13
  279.6 55.3 all-gather.15
  338.8 17.9 reduce-scatter.19
  378.3 17.4 reduce-scatter.21
  413.5 17.3 reduce-scatter.23
